TPU v7x, 32 devices: a whole 2x2x4 slice. The times are simulated.
32 devices in a mesh: lon: 8 (over y, x, core), lat: 4 (over z).
Axes of the slice: x: 2, y: 2, z: 4, core: 2. Of those that a mesh axis runs over, the one named last changes fastest.
Arguments:
- first_features: bfloat16 [32, 2048, 128], P(None, ('lon', 'lat')), may hold values from -6 to 6
- second_features: bfloat16 [32, 2048, 128], P(None, ('lon', 'lat')), may hold values from -6 to 6
- hidden_state: bfloat16 [32, 2048, 128], P('lat', 'lon'), may hold values from -1 to 1
- encoder_weight: bfloat16 [289, 128], replicated, may hold values from -0.375 to 0.375
- gates_weight: bfloat16 [3, 3, 256, 256], replicated, may hold values from -0.125 to 0.125
- candidate_weight: bfloat16 [3, 3, 256, 128], replicated, may hold values from -0.125 to 0.125
- row_metric: float32 [32], replicated, may hold values from 1 to 3
Outputs:
- new_state: bfloat16 [32, 2048, 128], P('lat', 'lon')
All inputs are finite; a program needn't handle non-finite values.
Results may differ from a plain program's by a relative error of at most 0.0058.
Values may be sent and summed in bfloat16 or wider, within the bound.
A program may use at most 64 MiB of HBM per device.

v0:
```python
import functools

import jax
import jax.numpy as jnp
from jax import lax
from jax.experimental import pallas as pl
from jax.experimental.pallas import tpu as pltpu
from jax.sharding import PartitionSpec as P

RADIUS = 8
WIN = 2 * RADIUS + 1
EDGE = 16
LANES = 128
SLOT = 24
PER_GROUP = LANES // SLOT
BF16 = jnp.bfloat16
F32 = jnp.float32


def copy_to(src, dst, sems, slot, lon, lat):
    return pltpu.make_async_remote_copy(
        src_ref=src,
        dst_ref=dst,
        send_sem=sems[0].at[slot],
        recv_sem=sems[1].at[slot],
        device_id={"lon": lon, "lat": lat},
        device_id_type=pl.DeviceIdType.MESH,
    )


def mirror(breadth):
    size = 2 * breadth
    total = lax.broadcasted_iota(jnp.int32, (size, size), 0)
    total += lax.broadcasted_iota(jnp.int32, (size, size), 1)
    return ((total == breadth - 1) | (total == 3 * breadth - 1)).astype(F32).astype(BF16)


def correlate_rows(pair, first, strips, encoder, motion):
    breadth = first.shape[1]
    left = first[pl.ds(2 * pair, 2)].reshape(2 * breadth, first.shape[2])
    groups = -(-WIN // PER_GROUP)
    packed = [[jnp.zeros((breadth, LANES), F32)] * groups for _ in range(2)]
    lane = lax.broadcasted_iota(jnp.int32, (breadth, LANES), 1)
    for step in range(0, WIN + 1, 2):
        right = strips[pl.ds(2 * pair + step, 2)].reshape(2 * LANES, first.shape[2])
        product = lax.dot_general(
            left, right, (((1,), (1,)), ((), ())), preferred_element_type=F32
        )
        for sub in range(2):
            for row in range(2):
                shift_y = step + sub - row
                if not 0 <= shift_y < WIN:
                    continue
                group, place = divmod(shift_y, PER_GROUP)
                band = product[
                    row * breadth : (row + 1) * breadth, sub * LANES : (sub + 1) * LANES
                ]
                start = SLOT * place
                turned = pltpu.roll(
                    band,
                    (start - (EDGE - RADIUS) - (breadth - 1)) % LANES,
                    1,
                    stride=1,
                    stride_axis=0,
                )
                inside = (lane >= start) & (lane < start + WIN)
                packed[row][group] = jnp.where(inside, turned, packed[row][group])
    scale = first.shape[2] ** (-0.5)
    rows = [jnp.concatenate(packed[row], axis=1) for row in range(2)]
    correlation = (jnp.concatenate(rows, axis=0) * scale).astype(BF16)
    out = jnp.dot(correlation, encoder[...], preferred_element_type=F32)
    out = jnp.maximum(out, 0.0).astype(BF16)
    out = jnp.dot(mirror(breadth), out, preferred_element_type=F32).astype(BF16)
    motion[pl.ds(2 * pair + 2, 2)] = out.reshape(2, breadth, -1)


def side_sum(west, east):
    span = west.shape[0]
    return pltpu.roll(west, 1, 0) + pltpu.roll(east, span - 1, 0)


def stacked(field, start, rows):
    span = field.shape[1]
    parts = [field[pl.ds(start + p, rows)].reshape(rows * span, -1) for p in range(3)]
    return parts


def interleave(a, b):
    return jnp.concatenate([part for both in zip(a, b) for part in both], axis=1)


def kernel(
    lats,
    lons,
    metric,
    first_hbm,
    second_hbm,
    hidden_hbm,
    encoder_in,
    gates_hbm,
    cand_hbm,
    out,
    first,
    strips,
    encoder,
    encoder_wide,
    encoder_slots,
    gates_w,
    cand_w,
    motion,
    hid,
    mot,
    reset,
    update,
    local_sems,
    second_sends,
    second_recvs,
    hid_sends,
    hid_recvs,
    mot_sends,
    mot_recvs,
    rim_sends,
    rim_recvs,
    west_recvs,
):
    height, breadth, channels = first.shape
    tile_rows, tile_cols = out.shape[0], out.shape[1]
    span = hid.shape[1]
    lon, lat = lax.axis_index("lon"), lax.axis_index("lat")
    east, west = lax.rem(lon + 1, lons), lax.rem(lon + lons - 1, lons)
    last = lats - 1

    locals_ = [
        (first_hbm, first),
        (second_hbm, strips.at[pl.ds(RADIUS, height), pl.ds(EDGE, breadth)]),
        (hidden_hbm, hid.at[pl.ds(2, tile_rows), pl.ds(EDGE, tile_cols)]),
        (gates_hbm, gates_w),
        (cand_hbm, cand_w),
    ]
    locals_ = [
        pltpu.make_async_copy(src, dst, local_sems.at[i]) for i, (src, dst) in enumerate(locals_)
    ]
    for copy in locals_:
        copy.start()

    zeros = functools.partial(jnp.zeros, dtype=BF16)
    strips[pl.ds(0, RADIUS)] = zeros((RADIUS, LANES, channels))
    strips[pl.ds(RADIUS + height, RADIUS)] = zeros((RADIUS, LANES, channels))
    used = breadth + 2 * EDGE
    if used < LANES:
        strips[pl.ds(RADIUS, height), pl.ds(used, LANES - used)] = zeros(
            (height, LANES - used, channels)
        )
    motion[pl.ds(0, 2)] = zeros((2, breadth, channels))
    motion[pl.ds(2 + height, 2)] = zeros((2, breadth, channels))

    @pl.when(lat == 0)
    def _():
        hid[pl.ds(0, 2)] = zeros((2, span, channels))

    @pl.when(lat == last)
    def _():
        hid[pl.ds(2 + tile_rows, 2)] = zeros((2, span, channels))

    barrier = pltpu.get_barrier_semaphore()
    peers = 0
    for group in (west, lon, east):
        for other in range(lats):
            if group is lon:
                if other == 0:
                    continue
                target = lax.rem(lat + other, lats)
            else:
                target = jnp.int32(other)
            pl.semaphore_signal(
                barrier,
                inc=1,
                device_id={"lon": group, "lat": target},
                device_id_type=pl.DeviceIdType.MESH,
            )
            peers += 1
    pl.semaphore_wait(barrier, peers)

    next_lat, prev_lat = lax.rem(lat + 1, lats), lax.rem(lat + last, lats)
    next_lon = lax.rem(lon + (lat + 1) // lats, lons)
    prev_lon = lax.rem(lon + lons - (lats - lat) // lats, lons)
    seconds = (second_sends, second_recvs)
    second_copies = [
        copy_to(
            second_hbm.at[:, pl.ds(breadth - EDGE, EDGE)],
            strips.at[pl.ds(RADIUS, height), pl.ds(0, EDGE)],
            seconds,
            0,
            next_lon,
            next_lat,
        ),
        copy_to(
            second_hbm.at[:, pl.ds(0, EDGE)],
            strips.at[pl.ds(RADIUS, height), pl.ds(EDGE + breadth, EDGE)],
            seconds,
            1,
            prev_lon,
            prev_lat,
        ),
    ]
    for copy in second_copies:
        copy.start()

    hids = (hid_sends, hid_recvs)
    sides = []
    slot = 0
    for dy in (-1, 0, 1):
        for dx in (-1, 0, 1):
            if dy == 0 and dx == 0:
                continue
            src_rows = {-1: pl.ds(0, 2), 0: pl.ds(0, tile_rows), 1: pl.ds(tile_rows - 2, 2)}[dy]
            dst_rows = {-1: pl.ds(2 + tile_rows, 2), 0: pl.ds(2, tile_rows), 1: pl.ds(0, 2)}[dy]
            src_cols = {
                -1: pl.ds(0, EDGE),
                0: pl.ds(0, tile_cols),
                1: pl.ds(tile_cols - EDGE, EDGE),
            }[dx]
            dst_cols = {
                -1: pl.ds(EDGE + tile_cols, EDGE),
                0: pl.ds(EDGE, tile_cols),
                1: pl.ds(0, EDGE),
            }[dx]
            to_lon = {-1: west, 0: lon, 1: east}[dx]
            to_lat = {-1: prev_lat, 0: lat, 1: next_lat}[dy]
            copy = copy_to(
                hidden_hbm.at[src_rows, src_cols],
                hid.at[dst_rows, dst_cols],
                hids,
                slot,
                to_lon,
                to_lat,
            )
            sends = {-1: lat > 0, 0: None, 1: lat < last}[dy]
            gets = {-1: lat < last, 0: None, 1: lat > 0}[dy]
            sides.append((copy, sends, gets))
            slot += 1

    def maybe(condition, action):
        if condition is None:
            action()
        else:
            pl.when(condition)(action)

    for copy, sends, gets in sides:
        maybe(sends, copy.start)

    encoder_wide[pl.ds(0, WIN * WIN)] = encoder_in[...].astype(F32)
    encoder_slots[...] = jnp.zeros(encoder_slots.shape, F32)
    for shift_y in range(WIN):
        group, place = divmod(shift_y, PER_GROUP)
        piece = encoder_wide[pl.ds(WIN * shift_y, SLOT)]
        row = lax.broadcasted_iota(jnp.int32, piece.shape, 0)
        target = pl.ds(group * LANES + SLOT * place, SLOT)
        encoder_slots[target] = jnp.where(row < WIN, piece, 0.0)
    encoder[...] = encoder_slots[...].astype(BF16)

    locals_[0].wait()

    def reverse(pair, carry):
        rows = first[pl.ds(2 * pair, 2)].reshape(2 * breadth, channels)
        rows = jnp.dot(mirror(breadth), rows, preferred_element_type=F32).astype(BF16)
        first[pl.ds(2 * pair, 2)] = rows.reshape(2, breadth, channels)
        return carry

    lax.fori_loop(0, height // 2, reverse, 0)
    locals_[1].wait()
    for copy in second_copies:
        copy.wait_recv()

    block = tile_rows + 4
    mots = (mot_sends, mot_recvs)
    rims = (rim_sends, rim_recvs)
    wests = (rim_sends, west_recvs)

    def slab_copy(dest):
        return pltpu.make_async_remote_copy(
            src_ref=motion.at[pl.ds(dest * tile_rows, block)],
            dst_ref=mot.at[:, pl.ds(pl.multiple_of(EDGE + lat * breadth, EDGE), breadth)],
            send_sem=mot_sends.at[dest],
            recv_sem=mot_recvs.at[lat],
            device_id={"lon": lon, "lat": jnp.int32(dest)},
            device_id_type=pl.DeviceIdType.MESH,
        )

    def own_copy(dest):
        return pltpu.make_async_copy(
            motion.at[pl.ds(dest * tile_rows, block)],
            mot.at[:, pl.ds(pl.multiple_of(EDGE + lat * breadth, EDGE), breadth)],
            mot_sends.at[dest],
        )

    def west_copy(dest):
        return pltpu.make_async_remote_copy(
            src_ref=motion.at[pl.ds(dest * tile_rows, block), pl.ds(0, EDGE)],
            dst_ref=mot.at[:, pl.ds(EDGE + tile_cols, EDGE)],
            send_sem=rim_sends.at[dest],
            recv_sem=rim_recvs.at[0],
            device_id={"lon": west, "lat": jnp.int32(dest)},
            device_id_type=pl.DeviceIdType.MESH,
        )

    def east_copy(dest):
        return pltpu.make_async_remote_copy(
            src_ref=motion.at[pl.ds(dest * tile_rows, block), pl.ds(breadth - EDGE, EDGE)],
            dst_ref=mot.at[:, pl.ds(0, EDGE)],
            send_sem=rim_sends.at[lats + dest],
            recv_sem=rim_recvs.at[1],
            device_id={"lon": east, "lat": jnp.int32(dest)},
            device_id_type=pl.DeviceIdType.MESH,
        )

    done = 0
    for dest in range(lats):
        upto = min(height, (dest + 1) * tile_rows + 2) // 2

        def step(pair, carry):
            correlate_rows(pair, first, strips, encoder, motion)
            return carry

        lax.fori_loop(done, upto, step, 0)
        done = upto
        maybe(lat == 0, west_copy(dest).start)
        maybe(lat == last, east_copy(dest).start)
        maybe(lat != dest, slab_copy(dest).start)
        maybe(lat == dest, own_copy(dest).start)

    locals_[2].wait()
    locals_[3].wait()
    locals_[4].wait()
    for copy, sends, gets in sides:
        maybe(gets, copy.wait_recv)

    for source in range(lats):
        arrived = pltpu.make_async_remote_copy(
            src_ref=motion.at[pl.ds(0, block)],
            dst_ref=mot.at[:, pl.ds(EDGE + source * breadth, breadth)],
            send_sem=mot_sends.at[source],
            recv_sem=mot_recvs.at[source],
            device_id={"lon": lon, "lat": jnp.int32(source)},
            device_id_type=pl.DeviceIdType.MESH,
        )
        maybe(lat != source, arrived.wait_recv)
        maybe(lat == source, own_copy(source).wait)
    west_copy(0).wait_recv()
    east_copy(0).wait_recv()

    def gate_rows(pair, carry):
        joined = interleave(stacked(hid, 2 * pair, 2), stacked(mot, 2 * pair, 2))
        sums = [
            jnp.dot(joined, gates_w[:, q].reshape(joined.shape[1], -1), preferred_element_type=F32)
            for q in range(3)
        ]
        for row in range(2):
            a, b, c = [s[row * span : (row + 1) * span] for s in sums]
            index = lax.rem(lat * tile_rows + 2 * pair + row + height - 1, height)
            values = jax.nn.sigmoid(b + side_sum(a, c) * metric[index])
            state = hid[2 * pair + row + 1].astype(F32)
            update[2 * pair + row] = values[:, :channels]
            reset[2 * pair + row] = (values[:, channels:] * state).astype(BF16)
        return carry

    lax.fori_loop(0, (tile_rows + 2) // 2, gate_rows, 0)

    def candidate_rows(pair, carry):
        joined = interleave(stacked(reset, 2 * pair, 2), stacked(mot, 2 * pair + 1, 2))
        weights = jnp.concatenate(
            [cand_w[:, q].reshape(joined.shape[1], -1) for q in range(3)], axis=1
        )
        sums = jnp.dot(joined, weights, preferred_element_type=F32)
        for row in range(2):
            part = sums[row * span : (row + 1) * span]
            a, b, c = [part[:, q * channels : (q + 1) * channels] for q in range(3)]
            index = lat * tile_rows + 2 * pair + row
            candidate = jnp.tanh(b + side_sum(a, c) * metric[index])
            gate = update[2 * pair + row + 1]
            state = hid[2 * pair + row + 2].astype(F32)
            new = (1.0 - gate) * state + gate * candidate
            out[2 * pair + row] = new[EDGE : EDGE + tile_cols].astype(BF16)
        return carry

    lax.fori_loop(0, tile_rows // 2, candidate_rows, 0)

    for copy in second_copies:
        copy.wait_send()
    for copy, sends, gets in sides:
        maybe(sends, copy.wait_send)
    for dest in range(lats):
        maybe(lat != dest, slab_copy(dest).wait_send)
        maybe(lat == 0, west_copy(dest).wait_send)
        maybe(lat == last, east_copy(dest).wait_send)


def body(lats, lons, first, second, hidden, encoder, gates, cand, row_metric):
    height, breadth, channels = first.shape
    tile_rows, tile_cols = hidden.shape[:2]
    span = tile_cols + 2 * EDGE
    groups = -(-WIN // PER_GROUP)
    hbm = pl.BlockSpec(memory_space=pl.ANY)
    vmem = pl.BlockSpec(memory_space=pltpu.VMEM)
    dma = pltpu.SemaphoreType.DMA
    return pl.pallas_call(
        functools.partial(kernel, lats, lons),
        out_shape=jax.ShapeDtypeStruct(hidden.shape, hidden.dtype),
        in_specs=[
            pl.BlockSpec(memory_space=pltpu.SMEM),
            hbm,
            hbm,
            hbm,
            vmem,
            hbm,
            hbm,
        ],
        out_specs=vmem,
        scratch_shapes=[
            pltpu.VMEM(first.shape, BF16),
            pltpu.VMEM((height + 2 * RADIUS, LANES, channels), BF16),
            pltpu.VMEM((groups * LANES, encoder.shape[1]), BF16),
            pltpu.VMEM((groups * LANES, encoder.shape[1]), F32),
            pltpu.VMEM((groups * LANES, encoder.shape[1]), F32),
            pltpu.VMEM(gates.shape, BF16),
            pltpu.VMEM(cand.shape, BF16),
            pltpu.VMEM((height + 4, breadth, channels), BF16),
            pltpu.VMEM((tile_rows + 4, span, channels), BF16),
            pltpu.VMEM((tile_rows + 4, span, channels), BF16),
            pltpu.VMEM((tile_rows + 2, span, channels), BF16),
            pltpu.VMEM((tile_rows + 2, span, channels), F32),
            dma((5,)),
            dma((2,)),
            dma((2,)),
            dma((8,)),
            dma((8,)),
            dma((lats,)),
            dma((lats,)),
            dma((2 * lats,)),
            dma((2,)),
            dma((2,)),
        ],
        compiler_params=pltpu.CompilerParams(
            collective_id=0, has_side_effects=True, vmem_limit_bytes=60 * 1024 * 1024
        ),
    )(row_metric, first, second, hidden, encoder, gates, cand)


def solution(mesh):
    return jax.shard_map(
        functools.partial(body, mesh.shape["lat"], mesh.shape["lon"]),
        mesh=mesh,
        in_specs=(
            P(None, ("lon", "lat"), None),
            P(None, ("lon", "lat"), None),
            P("lat", "lon", None),
            P(),
            P(),
            P(),
            P(),
        ),
        out_specs=P("lat", "lon", None),
        check_vma=False,
    )
```

profile of v0, /device:TPU:28, one launch (start us, length us, event | category | flops | bytes accessed | tf_op | source)
XLA Modules:
  0.0 52.6 jit_solution(14015701642416935301)
XLA Ops:
  0.0 50.7 %shard_map.73 = bf16[8,256,128]{2,1,0:T(8,128)(2,1)} custom-call(f32[32]{0:T(128)} %metric.1, bf16[32,64,128]{2,1,0:T(8,128)(2,1)} %first_hbm.1, bf16[32,64,128]{2,1,0:T(8,128)(2,1)} %second_hbm.1, bf16[8,256,128]{2,1,0:T(8,128)(2,1)} %hidden_hbm.1, bf16[289,128]{1,0:T(8,128)(2,1)} %encoder_in.1, bf16[3,3,256,256]{3,2,1,0:T(8,128)(2,1)} %gates_hbm.1, ...), custom_call_target="tpu_custom_call" | custom-call | tf_op jit(solution)/shard_map/pallas_call | solution.py:406
  50.7 1.9 %copy.9 = bf16[8,256,128]{2,1,0:T(8,128)(2,1)} copy(bf16[8,256,128]{2,1,0:T(8,128)(2,1)} %shard_map.73) | data formatting | bytes 1048576
where the time goes:
time: 52.8 us; the launch traced here: 52.6 us
  Pallas kernels  50.7 us (96%)
  local copies, waits for them, and re-layouts  1.87 us (4%)
    pallas_call x1, Pallas kernels, body(): pl.pallas_call(functools.partial(kernel, lats, lons), out_shape=jax.Shape...  50.7 us
    unnamed x1, local copies, waits for them, and re-layouts  1.87 us

commit v1 on v0

--- a/solution.py
+++ b/solution.py
@@ -10,6 +10,7 @@
 RADIUS = 8
 WIN = 2 * RADIUS + 1
 EDGE = 16
+HALO = 8
 LANES = 128
 SLOT = 24
 PER_GROUP = LANES // SLOT
@@ -71,7 +72,7 @@
     out = jnp.dot(correlation, encoder[...], preferred_element_type=F32)
     out = jnp.maximum(out, 0.0).astype(BF16)
     out = jnp.dot(mirror(breadth), out, preferred_element_type=F32).astype(BF16)
-    motion[pl.ds(2 * pair + 2, 2)] = out.reshape(2, breadth, -1)
+    motion[pl.ds(2 * pair, 2)] = out.reshape(2, breadth, -1)
 
 
 def side_sum(west, east):
@@ -112,6 +113,7 @@
     mot,
     reset,
     update,
+    state_sums,
     local_sems,
     second_sends,
     second_recvs,
@@ -121,7 +123,6 @@
     mot_recvs,
     rim_sends,
     rim_recvs,
-    west_recvs,
 ):
     height, breadth, channels = first.shape
     tile_rows, tile_cols = out.shape[0], out.shape[1]
@@ -146,21 +147,21 @@
     zeros = functools.partial(jnp.zeros, dtype=BF16)
     strips[pl.ds(0, RADIUS)] = zeros((RADIUS, LANES, channels))
     strips[pl.ds(RADIUS + height, RADIUS)] = zeros((RADIUS, LANES, channels))
-    used = breadth + 2 * EDGE
+    used = breadth + EDGE + HALO
     if used < LANES:
         strips[pl.ds(RADIUS, height), pl.ds(used, LANES - used)] = zeros(
             (height, LANES - used, channels)
         )
-    motion[pl.ds(0, 2)] = zeros((2, breadth, channels))
-    motion[pl.ds(2 + height, 2)] = zeros((2, breadth, channels))
 
     @pl.when(lat == 0)
     def _():
         hid[pl.ds(0, 2)] = zeros((2, span, channels))
+        mot[pl.ds(0, 2)] = zeros((2, span, channels))
 
     @pl.when(lat == last)
     def _():
         hid[pl.ds(2 + tile_rows, 2)] = zeros((2, span, channels))
+        mot[pl.ds(2 + tile_rows, 2)] = zeros((2, span, channels))
 
     barrier = pltpu.get_barrier_semaphore()
     peers = 0
@@ -187,16 +188,16 @@
     seconds = (second_sends, second_recvs)
     second_copies = [
         copy_to(
-            second_hbm.at[:, pl.ds(breadth - EDGE, EDGE)],
-            strips.at[pl.ds(RADIUS, height), pl.ds(0, EDGE)],
+            second_hbm.at[:, pl.ds(breadth - HALO, HALO)],
+            strips.at[pl.ds(RADIUS, height), pl.ds(EDGE - HALO, HALO)],
             seconds,
             0,
             next_lon,
             next_lat,
         ),
         copy_to(
-            second_hbm.at[:, pl.ds(0, EDGE)],
-            strips.at[pl.ds(RADIUS, height), pl.ds(EDGE + breadth, EDGE)],
+            second_hbm.at[:, pl.ds(0, HALO)],
+            strips.at[pl.ds(RADIUS, height), pl.ds(EDGE + breadth, HALO)],
             seconds,
             1,
             prev_lon,
@@ -216,14 +217,14 @@
             src_rows = {-1: pl.ds(0, 2), 0: pl.ds(0, tile_rows), 1: pl.ds(tile_rows - 2, 2)}[dy]
             dst_rows = {-1: pl.ds(2 + tile_rows, 2), 0: pl.ds(2, tile_rows), 1: pl.ds(0, 2)}[dy]
             src_cols = {
-                -1: pl.ds(0, EDGE),
+                -1: pl.ds(0, HALO),
                 0: pl.ds(0, tile_cols),
-                1: pl.ds(tile_cols - EDGE, EDGE),
+                1: pl.ds(tile_cols - HALO, HALO),
             }[dx]
             dst_cols = {
-                -1: pl.ds(EDGE + tile_cols, EDGE),
+                -1: pl.ds(EDGE + tile_cols, HALO),
                 0: pl.ds(EDGE, tile_cols),
-                1: pl.ds(0, EDGE),
+                1: pl.ds(EDGE - HALO, HALO),
             }[dx]
             to_lon = {-1: west, 0: lon, 1: east}[dx]
             to_lat = {-1: prev_lat, 0: lat, 1: next_lat}[dy]
@@ -246,9 +247,6 @@
         else:
             pl.when(condition)(action)
 
-    for copy, sends, gets in sides:
-        maybe(sends, copy.start)
-
     encoder_wide[pl.ds(0, WIN * WIN)] = encoder_in[...].astype(F32)
     encoder_slots[...] = jnp.zeros(encoder_slots.shape, F32)
     for shift_y in range(WIN):
@@ -271,63 +269,75 @@
     locals_[1].wait()
     for copy in second_copies:
         copy.wait_recv()
+    for copy, sends, gets in sides:
+        maybe(sends, copy.start)
 
     block = tile_rows + 4
-    mots = (mot_sends, mot_recvs)
-    rims = (rim_sends, rim_recvs)
-    wests = (rim_sends, west_recvs)
-
-    def slab_copy(dest):
+    flip = 1 - (2 * lat) // lats
+    slab_cols = pl.ds(pl.multiple_of(EDGE + lat * breadth, EDGE), breadth)
+
+    def blocks(dest):
+        top = dest * tile_rows
+        return [
+            (dest == 0, pl.ds(top, block - 2), pl.ds(2, block - 2)),
+            ((dest > 0) & (dest < last), pl.ds(top - 2, block), pl.ds(0, block)),
+            (dest == last, pl.ds(top - 2, block - 2), pl.ds(0, block - 2)),
+        ]
+
+    def slab_copy(dest, source, src_rows, dst_rows):
+        cols = pl.ds(pl.multiple_of(EDGE + source * breadth, EDGE), breadth)
         return pltpu.make_async_remote_copy(
-            src_ref=motion.at[pl.ds(dest * tile_rows, block)],
-            dst_ref=mot.at[:, pl.ds(pl.multiple_of(EDGE + lat * breadth, EDGE), breadth)],
+            src_ref=motion.at[src_rows],
+            dst_ref=mot.at[dst_rows, cols],
             send_sem=mot_sends.at[dest],
-            recv_sem=mot_recvs.at[lat],
-            device_id={"lon": lon, "lat": jnp.int32(dest)},
+            recv_sem=mot_recvs.at[source],
+            device_id={"lon": lon, "lat": dest},
             device_id_type=pl.DeviceIdType.MESH,
         )
 
-    def own_copy(dest):
+    def own_copy(src_rows, dst_rows):
         return pltpu.make_async_copy(
-            motion.at[pl.ds(dest * tile_rows, block)],
-            mot.at[:, pl.ds(pl.multiple_of(EDGE + lat * breadth, EDGE), breadth)],
-            mot_sends.at[dest],
-        )
-
-    def west_copy(dest):
+            motion.at[src_rows], mot.at[dst_rows, slab_cols], mot_sends.at[lat]
+        )
+
+    def west_copy(dest, src_rows, dst_rows):
         return pltpu.make_async_remote_copy(
-            src_ref=motion.at[pl.ds(dest * tile_rows, block), pl.ds(0, EDGE)],
-            dst_ref=mot.at[:, pl.ds(EDGE + tile_cols, EDGE)],
+            src_ref=motion.at[src_rows, pl.ds(0, HALO)],
+            dst_ref=mot.at[dst_rows, pl.ds(EDGE + tile_cols, HALO)],
             send_sem=rim_sends.at[dest],
             recv_sem=rim_recvs.at[0],
-            device_id={"lon": west, "lat": jnp.int32(dest)},
+            device_id={"lon": west, "lat": dest},
             device_id_type=pl.DeviceIdType.MESH,
         )
 
-    def east_copy(dest):
+    def east_copy(dest, src_rows, dst_rows):
         return pltpu.make_async_remote_copy(
-            src_ref=motion.at[pl.ds(dest * tile_rows, block), pl.ds(breadth - EDGE, EDGE)],
-            dst_ref=mot.at[:, pl.ds(0, EDGE)],
+            src_ref=motion.at[src_rows, pl.ds(breadth - HALO, HALO)],
+            dst_ref=mot.at[dst_rows, pl.ds(EDGE - HALO, HALO)],
             send_sem=rim_sends.at[lats + dest],
             recv_sem=rim_recvs.at[1],
-            device_id={"lon": east, "lat": jnp.int32(dest)},
+            device_id={"lon": east, "lat": dest},
             device_id_type=pl.DeviceIdType.MESH,
         )
 
+    pairs = height // 2
+
+    def step(index, carry):
+        pair = flip * (pairs - 1 - index) + (1 - flip) * index
+        correlate_rows(pair, first, strips, encoder, motion)
+        return carry
+
     done = 0
-    for dest in range(lats):
-        upto = min(height, (dest + 1) * tile_rows + 2) // 2
-
-        def step(pair, carry):
-            correlate_rows(pair, first, strips, encoder, motion)
-            return carry
-
+    for turn in range(lats):
+        upto = min(height, (turn + 1) * tile_rows + 2) // 2
         lax.fori_loop(done, upto, step, 0)
         done = upto
-        maybe(lat == 0, west_copy(dest).start)
-        maybe(lat == last, east_copy(dest).start)
-        maybe(lat != dest, slab_copy(dest).start)
-        maybe(lat == dest, own_copy(dest).start)
+        dest = flip * (last - turn) + (1 - flip) * turn
+        for here, src_rows, dst_rows in blocks(dest):
+            maybe(here & (lat != dest), slab_copy(dest, lat, src_rows, dst_rows).start)
+            maybe(here & (lat == dest), own_copy(src_rows, dst_rows).start)
+            maybe(here & (lat == 0), west_copy(dest, src_rows, dst_rows).start)
+            maybe(here & (lat == last), east_copy(dest, src_rows, dst_rows).start)
 
     locals_[2].wait()
     locals_[3].wait()
@@ -335,28 +345,33 @@
     for copy, sends, gets in sides:
         maybe(gets, copy.wait_recv)
 
-    for source in range(lats):
-        arrived = pltpu.make_async_remote_copy(
-            src_ref=motion.at[pl.ds(0, block)],
-            dst_ref=mot.at[:, pl.ds(EDGE + source * breadth, breadth)],
-            send_sem=mot_sends.at[source],
-            recv_sem=mot_recvs.at[source],
-            device_id={"lon": lon, "lat": jnp.int32(source)},
-            device_id_type=pl.DeviceIdType.MESH,
-        )
-        maybe(lat != source, arrived.wait_recv)
-        maybe(lat == source, own_copy(source).wait)
-    west_copy(0).wait_recv()
-    east_copy(0).wait_recv()
+    def state_rows(pair, carry):
+        fields = jnp.concatenate(stacked(hid, 2 * pair, 2), axis=1)
+        for q in range(3):
+            weights = gates_w[:, q, :channels].reshape(fields.shape[1], -1)
+            sums = jnp.dot(fields, weights, preferred_element_type=F32)
+            state_sums[q, pl.ds(2 * pair, 2)] = sums.reshape(2, span, -1)
+        return carry
+
+    lax.fori_loop(0, (tile_rows + 2) // 2, state_rows, 0)
+
+    for here, src_rows, dst_rows in blocks(lat):
+        for source in range(lats):
+            arrived = slab_copy(lat, jnp.int32(source), src_rows, dst_rows)
+            maybe(here & (lat != source), arrived.wait_recv)
+        maybe(here, own_copy(src_rows, dst_rows).wait)
+        maybe(here, west_copy(lat, src_rows, dst_rows).wait_recv)
+        maybe(here, east_copy(lat, src_rows, dst_rows).wait_recv)
 
     def gate_rows(pair, carry):
-        joined = interleave(stacked(hid, 2 * pair, 2), stacked(mot, 2 * pair, 2))
-        sums = [
-            jnp.dot(joined, gates_w[:, q].reshape(joined.shape[1], -1), preferred_element_type=F32)
-            for q in range(3)
-        ]
+        fields = jnp.concatenate(stacked(mot, 2 * pair, 2), axis=1)
+        sums = []
+        for q in range(3):
+            weights = gates_w[:, q, channels:].reshape(fields.shape[1], -1)
+            own = jnp.dot(fields, weights, preferred_element_type=F32)
+            sums.append(own.reshape(2, span, -1) + state_sums[q, pl.ds(2 * pair, 2)])
         for row in range(2):
-            a, b, c = [s[row * span : (row + 1) * span] for s in sums]
+            a, b, c = [s[row] for s in sums]
             index = lax.rem(lat * tile_rows + 2 * pair + row + height - 1, height)
             values = jax.nn.sigmoid(b + side_sum(a, c) * metric[index])
             state = hid[2 * pair + row + 1].astype(F32)
@@ -390,9 +405,11 @@
     for copy, sends, gets in sides:
         maybe(sends, copy.wait_send)
     for dest in range(lats):
-        maybe(lat != dest, slab_copy(dest).wait_send)
-        maybe(lat == 0, west_copy(dest).wait_send)
-        maybe(lat == last, east_copy(dest).wait_send)
+        dest = jnp.int32(dest)
+        for here, src_rows, dst_rows in blocks(dest):
+            maybe(here & (lat != dest), slab_copy(dest, lat, src_rows, dst_rows).wait_send)
+            maybe(here & (lat == 0), west_copy(dest, src_rows, dst_rows).wait_send)
+            maybe(here & (lat == last), east_copy(dest, src_rows, dst_rows).wait_send)
 
 
 def body(lats, lons, first, second, hidden, encoder, gates, cand, row_metric):
@@ -424,11 +441,12 @@
             pltpu.VMEM((groups * LANES, encoder.shape[1]), F32),
             pltpu.VMEM(gates.shape, BF16),
             pltpu.VMEM(cand.shape, BF16),
-            pltpu.VMEM((height + 4, breadth, channels), BF16),
+            pltpu.VMEM((height, breadth, channels), BF16),
             pltpu.VMEM((tile_rows + 4, span, channels), BF16),
             pltpu.VMEM((tile_rows + 4, span, channels), BF16),
             pltpu.VMEM((tile_rows + 2, span, channels), BF16),
             pltpu.VMEM((tile_rows + 2, span, channels), F32),
+            pltpu.VMEM((3, tile_rows + 2, span, gates.shape[-1]), F32),
             dma((5,)),
             dma((2,)),
             dma((2,)),
@@ -437,7 +455,6 @@
             dma((lats,)),
             dma((lats,)),
             dma((2 * lats,)),
-            dma((2,)),
             dma((2,)),
         ],
         compiler_params=pltpu.CompilerParams(

time: 52.8 us -> 40.2 us (0.76)
  the two profiles are of different devices: /device:TPU:28 before, /device:TPU:12 now
where the time goes in v1:
time: 40.2 us; the launch traced here: 40 us
  Pallas kernels  38.2 us (95%)
  local copies, waits for them, and re-layouts  1.87 us (5%)
    pallas_call x1, Pallas kernels, body(): pl.pallas_call(functools.partial(kernel, lats, lons), out_shape=jax.Shape...  38.2 us
    unnamed x1, local copies, waits for them, and re-layouts  1.87 us

profile of v1, /device:TPU:12, one launch (start us, length us, event | category | flops | bytes accessed | tf_op | source)
XLA Modules:
  0.0 40.0 jit_solution(1901423884487836119)
XLA Ops:
  0.0 38.2 %shard_map.73 = bf16[8,256,128]{2,1,0:T(8,128)(2,1)} custom-call(f32[32]{0:T(128)} %metric.1, bf16[32,64,128]{2,1,0:T(8,128)(2,1)} %first_hbm.1, bf16[32,64,128]{2,1,0:T(8,128)(2,1)} %second_hbm.1, bf16[8,256,128]{2,1,0:T(8,128)(2,1)} %hidden_hbm.1, bf16[289,128]{1,0:T(8,128)(2,1)} %encoder_in.1, bf16[3,3,256,256]{3,2,1,0:T(8,128)(2,1)} %gates_hbm.1, ...), custom_call_target="tpu_custom_call" | custom-call | tf_op jit(solution)/shard_map/pallas_call | solution.py:423
  38.2 1.9 %copy.9 = bf16[8,256,128]{2,1,0:T(8,128)(2,1)} copy(bf16[8,256,128]{2,1,0:T(8,128)(2,1)} %shard_map.73) | data formatting | bytes 1048576

commit v2 on v1

--- a/solution.py
+++ b/solution.py
@@ -86,10 +86,6 @@
     return parts
 
 
-def interleave(a, b):
-    return jnp.concatenate([part for both in zip(a, b) for part in both], axis=1)
-
-
 def kernel(
     lats,
     lons,
@@ -114,6 +110,7 @@
     reset,
     update,
     state_sums,
+    cand_sums,
     local_sems,
     second_sends,
     second_recvs,
@@ -355,40 +352,77 @@
 
     lax.fori_loop(0, (tile_rows + 2) // 2, state_rows, 0)
 
+    def columns_sum(cols_list):
+        def taps(first_row, rows):
+            taken = [
+                [mot[pl.ds(first_row + p, rows), cols] for p in range(3)] for cols in cols_list
+            ]
+            flat = [
+                jnp.concatenate([t.reshape(-1, channels) for t in three], axis=1)
+                for three in taken
+            ]
+            return jnp.concatenate(flat, axis=0)
+
+        def split(sums, rows):
+            share = sums.shape[0] // len(cols_list)
+            return [
+                sums[i * share : (i + 1) * share].reshape(rows, share // rows, -1)
+                for i in range(len(cols_list))
+            ]
+
+        fields = taps(0, tile_rows + 2)
+        for q in range(3):
+            weights = gates_w[:, q, channels:].reshape(fields.shape[1], -1)
+            sums = jnp.dot(fields, weights, preferred_element_type=F32)
+            for cols, part in zip(cols_list, split(sums, tile_rows + 2)):
+                state_sums[q, :, cols] += part
+        fields = taps(1, tile_rows)
+        weights = jnp.concatenate(
+            [cand_w[:, q, channels:].reshape(fields.shape[1], -1) for q in range(3)], axis=1
+        )
+        sums = jnp.dot(fields, weights, preferred_element_type=F32)
+        for cols, part in zip(cols_list, split(sums, tile_rows)):
+            cand_sums[:, cols] = part
+
+    def slab_sum(turn, carry):
+        half = max(lats // 2, 1)
+        mine = (lat // half) * half
+        other = lats - half - mine
+        near = mine + lax.rem(lat + turn, half)
+        far = other + lax.rem(lat + turn, half)
+        beyond = turn // half
+        source = near * (1 - beyond) + far * beyond
+        for here, src_rows, dst_rows in blocks(lat):
+            maybe(here & (turn == 0), own_copy(src_rows, dst_rows).wait)
+            maybe(here & (turn > 0), slab_copy(lat, source, src_rows, dst_rows).wait_recv)
+        columns_sum([pl.ds(pl.multiple_of(EDGE + source * breadth, EDGE), breadth)])
+        return carry
+
+    lax.fori_loop(0, lats - 1, slab_sum, 0)
     for here, src_rows, dst_rows in blocks(lat):
-        for source in range(lats):
-            arrived = slab_copy(lat, jnp.int32(source), src_rows, dst_rows)
-            maybe(here & (lat != source), arrived.wait_recv)
-        maybe(here, own_copy(src_rows, dst_rows).wait)
         maybe(here, west_copy(lat, src_rows, dst_rows).wait_recv)
         maybe(here, east_copy(lat, src_rows, dst_rows).wait_recv)
-
-    def gate_rows(pair, carry):
-        fields = jnp.concatenate(stacked(mot, 2 * pair, 2), axis=1)
-        sums = []
-        for q in range(3):
-            weights = gates_w[:, q, channels:].reshape(fields.shape[1], -1)
-            own = jnp.dot(fields, weights, preferred_element_type=F32)
-            sums.append(own.reshape(2, span, -1) + state_sums[q, pl.ds(2 * pair, 2)])
+    columns_sum([pl.ds(0, EDGE), pl.ds(EDGE + tile_cols, EDGE)])
+    lax.fori_loop(lats - 1, lats, slab_sum, 0)
+
+    def gate_rows(line, carry):
+        a, b, c = [state_sums[q, line] for q in range(3)]
+        index = lax.rem(lat * tile_rows + line + height - 1, height)
+        values = jax.nn.sigmoid(b + side_sum(a, c) * metric[index])
+        update[line] = values[:, :channels]
+        reset[line] = (values[:, channels:] * hid[line + 1].astype(F32)).astype(BF16)
+        return carry
+
+    lax.fori_loop(0, tile_rows + 2, gate_rows, 0)
+
+    def candidate_rows(pair, carry):
+        fields = jnp.concatenate(stacked(reset, 2 * pair, 2), axis=1)
+        weights = jnp.concatenate(
+            [cand_w[:, q, :channels].reshape(fields.shape[1], -1) for q in range(3)], axis=1
+        )
+        sums = jnp.dot(fields, weights, preferred_element_type=F32)
         for row in range(2):
-            a, b, c = [s[row] for s in sums]
-            index = lax.rem(lat * tile_rows + 2 * pair + row + height - 1, height)
-            values = jax.nn.sigmoid(b + side_sum(a, c) * metric[index])
-            state = hid[2 * pair + row + 1].astype(F32)
-            update[2 * pair + row] = values[:, :channels]
-            reset[2 * pair + row] = (values[:, channels:] * state).astype(BF16)
-        return carry
-
-    lax.fori_loop(0, (tile_rows + 2) // 2, gate_rows, 0)
-
-    def candidate_rows(pair, carry):
-        joined = interleave(stacked(reset, 2 * pair, 2), stacked(mot, 2 * pair + 1, 2))
-        weights = jnp.concatenate(
-            [cand_w[:, q].reshape(joined.shape[1], -1) for q in range(3)], axis=1
-        )
-        sums = jnp.dot(joined, weights, preferred_element_type=F32)
-        for row in range(2):
-            part = sums[row * span : (row + 1) * span]
+            part = sums[row * span : (row + 1) * span] + cand_sums[2 * pair + row]
             a, b, c = [part[:, q * channels : (q + 1) * channels] for q in range(3)]
             index = lat * tile_rows + 2 * pair + row
             candidate = jnp.tanh(b + side_sum(a, c) * metric[index])
@@ -447,6 +481,7 @@
             pltpu.VMEM((tile_rows + 2, span, channels), BF16),
             pltpu.VMEM((tile_rows + 2, span, channels), F32),
             pltpu.VMEM((3, tile_rows + 2, span, gates.shape[-1]), F32),
+            pltpu.VMEM((tile_rows, span, 3 * cand.shape[-1]), F32),
             dma((5,)),
             dma((2,)),
             dma((2,)),

time: 40.2 us -> 39.7 us (0.988)
  the two profiles are of different devices: /device:TPU:12 before, /device:TPU:19 now
where the time goes in v2:
time: 39.7 us; the launch traced here: 39.5 us
  Pallas kernels  37.6 us (95%)
  local copies, waits for them, and re-layouts  1.87 us (5%)
    pallas_call x1, Pallas kernels, body(): pl.pallas_call(functools.partial(kernel, lats, lons), out_shape=jax.Shape...  37.6 us
    unnamed x1, local copies, waits for them, and re-layouts  1.87 us

profile of v2, /device:TPU:19, one launch (start us, length us, event | category | flops | bytes accessed | tf_op | source)
XLA Modules:
  0.0 39.5 jit_solution(15192700708601022479)
XLA Ops:
  0.0 37.6 %shard_map.73 = bf16[8,256,128]{2,1,0:T(8,128)(2,1)} custom-call(f32[32]{0:T(128)} %metric.1, bf16[32,64,128]{2,1,0:T(8,128)(2,1)} %first_hbm.1, bf16[32,64,128]{2,1,0:T(8,128)(2,1)} %second_hbm.1, bf16[8,256,128]{2,1,0:T(8,128)(2,1)} %hidden_hbm.1, bf16[289,128]{1,0:T(8,128)(2,1)} %encoder_in.1, bf16[3,3,256,256]{3,2,1,0:T(8,128)(2,1)} %gates_hbm.1, ...), custom_call_target="tpu_custom_call" | custom-call | tf_op jit(solution)/shard_map/pallas_call | solution.py:457
  37.6 1.9 %copy.9 = bf16[8,256,128]{2,1,0:T(8,128)(2,1)} copy(bf16[8,256,128]{2,1,0:T(8,128)(2,1)} %shard_map.73) | data formatting | bytes 1048576

commit v3 on v2

--- a/solution.py
+++ b/solution.py
@@ -281,20 +281,35 @@
             (dest == last, pl.ds(top - 2, block - 2), pl.ds(0, block - 2)),
         ]
 
-    def slab_copy(dest, source, src_rows, dst_rows):
+    half_block = block // 2
+
+    def pieces(dest, part):
+        rim = ((dest == 0) & (part == 0)) | ((dest == last) & (part == 1))
+        kept = half_block - 2
+        top = dest * tile_rows
+        return [
+            (rim, pl.ds(top + kept * part, kept), pl.ds(2 + kept * part, kept)),
+            (
+                jnp.logical_not(rim),
+                pl.ds(top - 2 + half_block * part, half_block),
+                pl.ds(half_block * part, half_block),
+            ),
+        ]
+
+    def slab_copy(dest, source, part, src_rows, dst_rows):
         cols = pl.ds(pl.multiple_of(EDGE + source * breadth, EDGE), breadth)
         return pltpu.make_async_remote_copy(
             src_ref=motion.at[src_rows],
             dst_ref=mot.at[dst_rows, cols],
-            send_sem=mot_sends.at[dest],
-            recv_sem=mot_recvs.at[source],
+            send_sem=mot_sends.at[2 * dest + part],
+            recv_sem=mot_recvs.at[2 * source + part],
             device_id={"lon": lon, "lat": dest},
             device_id_type=pl.DeviceIdType.MESH,
         )
 
     def own_copy(src_rows, dst_rows):
         return pltpu.make_async_copy(
-            motion.at[src_rows], mot.at[dst_rows, slab_cols], mot_sends.at[lat]
+            motion.at[src_rows], mot.at[dst_rows, slab_cols], mot_sends.at[2 * lat]
         )
 
     def west_copy(dest, src_rows, dst_rows):
@@ -326,12 +341,18 @@
 
     done = 0
     for turn in range(lats):
-        upto = min(height, (turn + 1) * tile_rows + 2) // 2
-        lax.fori_loop(done, upto, step, 0)
-        done = upto
         dest = flip * (last - turn) + (1 - flip) * turn
+        for order, ready in enumerate(
+            (turn * tile_rows + half_block - 2, (turn + 1) * tile_rows + 2)
+        ):
+            upto = min(pairs, (ready + 1) // 2)
+            lax.fori_loop(done, upto, step, 0)
+            done = upto
+            part = flip * (1 - order) + (1 - flip) * order
+            for here, src_rows, dst_rows in pieces(dest, part):
+                copy = slab_copy(dest, lat, part, src_rows, dst_rows)
+                maybe(here & (lat != dest), copy.start)
         for here, src_rows, dst_rows in blocks(dest):
-            maybe(here & (lat != dest), slab_copy(dest, lat, src_rows, dst_rows).start)
             maybe(here & (lat == dest), own_copy(src_rows, dst_rows).start)
             maybe(here & (lat == 0), west_copy(dest, src_rows, dst_rows).start)
             maybe(here & (lat == last), east_copy(dest, src_rows, dst_rows).start)
@@ -394,7 +415,10 @@
         source = near * (1 - beyond) + far * beyond
         for here, src_rows, dst_rows in blocks(lat):
             maybe(here & (turn == 0), own_copy(src_rows, dst_rows).wait)
-            maybe(here & (turn > 0), slab_copy(lat, source, src_rows, dst_rows).wait_recv)
+        for part in range(2):
+            for here, src_rows, dst_rows in pieces(lat, part):
+                copy = slab_copy(lat, source, part, src_rows, dst_rows)
+                maybe(here & (turn > 0), copy.wait_recv)
         columns_sum([pl.ds(pl.multiple_of(EDGE + source * breadth, EDGE), breadth)])
         return carry
 
@@ -408,7 +432,7 @@
     def gate_rows(line, carry):
         a, b, c = [state_sums[q, line] for q in range(3)]
         index = lax.rem(lat * tile_rows + line + height - 1, height)
-        values = jax.nn.sigmoid(b + side_sum(a, c) * metric[index])
+        values = 0.5 + 0.5 * jnp.tanh(0.5 * (b + side_sum(a, c) * metric[index]))
         update[line] = values[:, :channels]
         reset[line] = (values[:, channels:] * hid[line + 1].astype(F32)).astype(BF16)
         return carry
@@ -440,8 +464,11 @@
         maybe(sends, copy.wait_send)
     for dest in range(lats):
         dest = jnp.int32(dest)
+        for part in range(2):
+            for here, src_rows, dst_rows in pieces(dest, part):
+                copy = slab_copy(dest, lat, part, src_rows, dst_rows)
+                maybe(here & (lat != dest), copy.wait_send)
         for here, src_rows, dst_rows in blocks(dest):
-            maybe(here & (lat != dest), slab_copy(dest, lat, src_rows, dst_rows).wait_send)
             maybe(here & (lat == 0), west_copy(dest, src_rows, dst_rows).wait_send)
             maybe(here & (lat == last), east_copy(dest, src_rows, dst_rows).wait_send)
 
@@ -487,8 +514,8 @@
             dma((2,)),
             dma((8,)),
             dma((8,)),
-            dma((lats,)),
-            dma((lats,)),
+            dma((2 * lats,)),
+            dma((2 * lats,)),
             dma((2 * lats,)),
             dma((2,)),
         ],

time: 39.7 us -> 39.2 us (0.987)
  Pallas kernels: 37.6 us -> 37.1 us
    pallas_call x1, Pallas kernels: 37.6 us -> 37.1 us  [body(): pl.pallas_call(functools.partial(kernel, lats, lons), out_shape=jax.Shape...]
where the time goes in v3:
time: 39.2 us; the launch traced here: 39 us
  Pallas kernels  37.1 us (95%)
  local copies, waits for them, and re-layouts  1.87 us (5%)
    pallas_call x1, Pallas kernels, body(): pl.pallas_call(functools.partial(kernel, lats, lons), out_shape=jax.Shape...  37.1 us
    unnamed x1, local copies, waits for them, and re-layouts  1.87 us

profile of v3, /device:TPU:19, one launch (start us, length us, event | category | flops | bytes accessed | tf_op | source)
XLA Modules:
  0.0 39.0 jit_solution(16122879956236951470)
XLA Ops:
  0.0 37.1 %shard_map.73 = bf16[8,256,128]{2,1,0:T(8,128)(2,1)} custom-call(f32[32]{0:T(128)} %metric.1, bf16[32,64,128]{2,1,0:T(8,128)(2,1)} %first_hbm.1, bf16[32,64,128]{2,1,0:T(8,128)(2,1)} %second_hbm.1, bf16[8,256,128]{2,1,0:T(8,128)(2,1)} %hidden_hbm.1, bf16[289,128]{1,0:T(8,128)(2,1)} %encoder_in.1, bf16[3,3,256,256]{3,2,1,0:T(8,128)(2,1)} %gates_hbm.1, ...), custom_call_target="tpu_custom_call" | custom-call | tf_op jit(solution)/shard_map/pallas_call | solution.py:484
  37.1 1.9 %copy.9 = bf16[8,256,128]{2,1,0:T(8,128)(2,1)} copy(bf16[8,256,128]{2,1,0:T(8,128)(2,1)} %shard_map.73) | data formatting | bytes 1048576
